TPU v7x, 256 devices: a whole 4x4x8 slice. The times are simulated.
256 devices in a mesh: brick: 8 (over x_lo, y), bulk: 32 (over x_hi, z, core).
Axes of the slice: x: 4 (x_hi: 2, x_lo: 2; x = x_hi * 2 + x_lo), y: 4, z: 8, core: 2. Of those that a mesh axis runs over, the one named last changes fastest.
Arguments:
- amp_traces: float32 [128, 2048, 256], P(None, ('bulk', 'brick')), may hold values from -6 to 6
- patch_owner: int32 [524288, 1], P(('brick', 'bulk')), may hold values from 0 to 31; in each aligned block of 2048 rows (0 to 2047, 2048 to 4095, ...) at most 256 rows name the same one
- patch_fault: int32 [524288], P(('brick', 'bulk')), may hold values from 0 to 15
- patch_trace: int32 [524288], P(('brick', 'bulk')), may hold values from 0 to 1023
- patch_offset: int32 [524288], P(('brick', 'bulk')), may hold values from 0 to 128
Outputs:
- fault_attr: float32 [128, 2048, 256], P('brick', 'bulk')
- fault_profile: float32 [4096, 128], P(('brick', 'bulk'))
Inputs may be any that keep to these rules, and one draw needn't show every extreme that they name: `patch_owner`: among the 2048 patches of one device, at most 256 name the same owner, and in every draw some device has exactly 256 patches with one owner.
All inputs are finite; a program needn't handle non-finite values.
Results may differ from a plain program's by a relative error of at most 0.0003.
Values sent between devices are 32-bit elements; how exact they have to be, the bound alone decides.
A program may use at most 64 MiB of HBM per device.

v0:
```python
import jax
import jax.numpy as jnp
from jax import lax
from jax.sharding import PartitionSpec as P

PATCH = 128
F_DEV = 16


def padded_2(block, sides, width):
    for axis, dim in sides:
        count = lax.axis_size(axis)
        forward = [(i, i + 1) for i in range(count - 1)]
        backward = [(target, source) for source, target in forward]
        low = lax.ppermute(
            lax.slice_in_dim(block, block.shape[dim] - width, None, axis=dim), axis, forward
        )
        high = lax.ppermute(lax.slice_in_dim(block, 0, width, axis=dim), axis, backward)
        block = jnp.concatenate([low, block, high], axis=dim)
    return block


def box_sum(values, radius, dimension):
    length = values.shape[dimension] - 2 * radius
    summed = lax.slice_in_dim(values, 0, length, axis=dimension)
    for offset in range(1, 2 * radius + 1):
        summed = summed + lax.slice_in_dim(values, offset, offset + length, axis=dimension)
    return summed


def time_sum(values, radius):
    widths = [(0, 0)] * (values.ndim - 1) + [(radius, radius)]
    return box_sum(jnp.pad(values, widths), radius, values.ndim - 1)


def gradient_energy(padded):
    slope_inline = 0.5 * (padded[2:, 1:-1, :] - padded[:-2, 1:-1, :])
    slope_cross = 0.5 * (padded[1:-1, 2:, :] - padded[1:-1, :-2, :])
    centre = jnp.pad(padded[1:-1, 1:-1, :], ((0, 0), (0, 0), (1, 1)))
    slope_time = 0.5 * (centre[:, :, 2:] - centre[:, :, :-2])
    return jnp.stack(
        [slope_inline * slope_inline, slope_cross * slope_cross, slope_time * slope_time]
    )


def smooth_tensor(energy):
    return time_sum(box_sum(box_sum(energy, 2, 1), 2, 2), 2)


def finish(tensor, near_amp):
    lateral = (tensor[0] + tensor[1]) / (tensor[0] + tensor[1] + tensor[2] + 1e-05)
    stack = box_sum(box_sum(near_amp, 1, 0), 1, 1)
    power = box_sum(box_sum(near_amp * near_amp, 1, 0), 1, 1)
    semblance = time_sum(stack * stack, 4) / (9.0 * time_sum(power, 4) + 1e-05)
    return (1.0 - semblance) * lateral


def window_rows(chosen, offsets, width):
    samples = chosen.shape[1]
    steps = (samples - width).bit_length()
    current = chosen
    for level in range(steps):
        amount = 1 << level
        moved = jnp.concatenate(
            [current[:, amount:], jnp.zeros((current.shape[0], amount), current.dtype)], axis=1
        )
        taken = (offsets >> level & 1)[:, None] == 1
        current = jnp.where(taken, moved, current)
    return current[:, :width]


def local(amp_traces, patch_owner, patch_fault, patch_trace, patch_offset):
    bricked = lax.all_to_all(amp_traces, "brick", split_axis=0, concat_axis=1, tiled=True)
    near_amp = padded_2(bricked, (("brick", 0), ("bulk", 1)), 1)
    energy = gradient_energy(near_amp)
    rimmed = padded_2(energy, (("brick", 1), ("bulk", 2)), 2)
    attribute = finish(smooth_tensor(rimmed), near_amp)
    flattened = attribute.reshape(-1, attribute.shape[2])
    chosen = flattened[patch_trace]
    patch_rows = window_rows(chosen, patch_offset, PATCH)
    owners = patch_owner[:, 0]
    owner_count = lax.axis_size("bulk")
    count_patches = patch_rows.shape[0]
    one_hot = (owners[:, None] == jnp.arange(owner_count, dtype=jnp.int32)[None, :]).astype(
        jnp.int32
    )
    placed = jnp.cumsum(one_hot, axis=0)
    slot_rank = jnp.sum(placed * one_hot, axis=1) - 1
    capacity = 4 * count_patches // owner_count
    buffer = (
        jnp.zeros((owner_count, capacity, PATCH), jnp.float32).at[owners, slot_rank].set(patch_rows)
    )
    labels = (
        jnp.zeros((owner_count, capacity), jnp.float32)
        .at[owners, slot_rank]
        .set(patch_fault.astype(jnp.float32) + 1.0)
    )
    got_rows, got_labels = (
        lax.all_to_all(buffer, "bulk", split_axis=0, concat_axis=0, tiled=True),
        lax.all_to_all(labels, "bulk", split_axis=0, concat_axis=0, tiled=True),
    )
    wanted = jnp.arange(F_DEV, dtype=jnp.float32) + 1.0
    selector = (got_labels.reshape(1, -1) == wanted[:, None]).astype(jnp.float32)
    summed = jnp.dot(
        selector,
        got_rows.reshape(-1, PATCH),
        precision=lax.Precision.HIGHEST,
        preferred_element_type=jnp.float32,
    )
    counts = jnp.sum(selector, axis=1)
    profile = summed / jnp.maximum(counts, 1.0)[:, None]
    return (attribute, profile)


def solution(mesh):
    in_specs = (
        P(None, ("bulk", "brick"), None),
        P(("brick", "bulk"), None),
        P(("brick", "bulk")),
        P(("brick", "bulk")),
        P(("brick", "bulk")),
    )
    out_specs = (P("brick", "bulk", None), P(("brick", "bulk"), None))
    return jax.shard_map(local, mesh=mesh, in_specs=in_specs, out_specs=out_specs, check_vma=False)
```

profile of v0, /device:TPU:1, one launch (start us, length us, event | category | flops | bytes accessed | tf_op | source)
XLA Modules:
  0.0 230.0 jit_solution(7785057367832346467)
XLA Ops:
  0.7 6.1 %all-to-all-start = ((f32[128,8,256]{2,1,0:T(8,128)}), f32[128,8,256]{2,1,0:T(8,128)S(1)}, u32[]{:S(2)}, u32[]{:S(2)}) async-start(f32[128,8,256]{2,1,0:T(8,128)} %param.5), calls=%async_computation | async-start | bytes 2097152 | tf_op jit(solution)/shard_map/all_to_all | solution.py:73
  6.8 9.1 %reduce-window.6 = s32[32,16,128]{2,1,0:T(8,128)S(1)} reduce-window(s32[32,16,128]{2,1,0:T(8,128)S(1)} %fusion.51, s32[]{:T(128)} %constant.22.clone.1), window={size=1x1x128 pad=0_0x0_0x127_0}, to_apply=%region_0.1 | reduce-window | flops 8323072 | bytes 524292 | tf_op jit(solution)/shard_map/reduce-window
  17.0 8.6 %scatter_custom_fusion = f32[8192]{0:T(1024)} fusion(s32[2048]{0:T(1024)S(1)} %broadcast_select_fusion, f32[2048]{0:T(1024)S(1)} %convert_add_fusion, f32[]{:T(128)} %constant.18.clone.1), kind=kCustom, calls=%fused_computation.139 | custom fusion | bytes 32772
  25.6 11.7 %all-to-all-start.1 = ((f32[32,1,256]{2,1,0:T(1,128)}), f32[32,1,256]{2,1,0:T(1,128)S(1)}, u32[]{:S(2)}, u32[]{:S(2)}) async-start(f32[32,1,256]{2,1,0:T(1,128)} %bitcast.18), calls=%async_computation.1 | async-start | bytes 65536 | tf_op jit(solution)/shard_map/all_to_all | solution.py:100
  37.5 3.6 %collective-permute-start = (f32[1,64,256]{2,1,0:T(8,128)S(1)}, f32[1,64,256]{2,1,0:T(8,128)S(1)}, u32[]{:S(2)}, u32[]{:S(2)}) collective-permute-start(f32[1,64,256]{2,1,0:T(8,128)S(1)} %get-tuple-element.13), channel_id=1, source_target_pairs={{0,32},{32,64},{64,96},{96,128},{128,160},{160,192},{192,224},{1,3... | collective-permute-start | bytes 196616 | tf_op jit(solution)/shard_map/ppermute | solution.py:15
  41.1 1.3 collective-permute-start.1
  42.5 4.0 %collective-permute-done.1 = f32[1,64,256]{2,1,0:T(8,128)S(1)} collective-permute-done((f32[1,64,256]{2,1,0:T(8,128)S(1)}, f32[1,64,256]{2,1,0:T(8,128)S(1)}, u32[]{:S(2)}, u32[]{:S(2)}) %collective-permute-start.1) | collective-permute-done | bytes 65568 | tf_op jit(solution)/shard_map/ppermute | solution.py:18
  46.5 4.7 %collective-permute-start.2 = (f32[18,1,256]{2,1,0:T(1,128)S(1)}, f32[18,1,256]{2,1,0:T(1,128)S(1)}, u32[]{:S(2)}, u32[]{:S(2)}) collective-permute-start(f32[18,1,256]{2,1,0:T(1,128)S(1)} %get-tuple-element.11), channel_id=1, source_target_pairs={{0,1},{1,2},{2,3},{3,4},{4,5},{5,6},{6,7},{7,8},{8,9},{9,10},{10,1... | collective-permute-start | bytes 55304 | tf_op jit(solution)/shard_map/ppermute | solution.py:15
  51.2 1.9 collective-permute-start.3
  53.1 3.1 %collective-permute-done.3 = f32[18,1,256]{2,1,0:T(1,128)S(1)} collective-permute-done((f32[18,1,256]{2,1,0:T(1,128)S(1)}, f32[18,1,256]{2,1,0:T(1,128)S(1)}, u32[]{:S(2)}, u32[]{:S(2)}) %collective-permute-start.3) | collective-permute-done | bytes 18464 | tf_op jit(solution)/shard_map/ppermute | solution.py:18
  56.2 0.9 fusion.42
  57.2 3.1 %collective-permute-start.4 = (f32[3,2,64,256]{3,2,1,0:T(8,128)S(1)}, f32[3,2,64,256]{3,2,1,0:T(8,128)S(1)}, u32[]{:S(2)}, u32[]{:S(2)}) collective-permute-start(f32[3,2,64,256]{3,2,1,0:T(8,128)S(1)} %get-tuple-element.4), channel_id=1, source_target_pairs={{0,32},{32,64},{64,96},{96,128},{128,160},{160,192},{192,224},{1,3... | collective-permute-start | bytes 1179656 | tf_op jit(solution)/shard_map/ppermute | solution.py:15
  60.3 1.3 collective-permute-start.5
  62.3 5.4 %collective-permute-done.4 = f32[3,2,64,256]{3,2,1,0:T(8,128)S(1)} collective-permute-done((f32[3,2,64,256]{3,2,1,0:T(8,128)S(1)}, f32[3,2,64,256]{3,2,1,0:T(8,128)S(1)}, u32[]{:S(2)}, u32[]{:S(2)}) %collective-permute-start.4) | collective-permute-done | bytes 393248 | tf_op jit(solution)/shard_map/ppermute | solution.py:15
  67.7 4.1 %collective-permute-done.5 = f32[3,2,64,256]{3,2,1,0:T(8,128)S(1)} collective-permute-done((f32[3,2,64,256]{3,2,1,0:T(8,128)S(1)}, f32[3,2,64,256]{3,2,1,0:T(8,128)S(1)}, u32[]{:S(2)}, u32[]{:S(2)}) %collective-permute-start.5) | collective-permute-done | bytes 393248 | tf_op jit(solution)/shard_map/ppermute | solution.py:18
  71.9 4.3 %collective-permute-start.6 = (f32[3,20,2,256]{3,2,1,0:T(2,128)S(1)}, f32[3,20,2,256]{3,2,1,0:T(2,128)S(1)}, u32[]{:S(2)}, u32[]{:S(2)}) collective-permute-start(f32[3,20,2,256]{3,2,1,0:T(2,128)S(1)} %get-tuple-element.2), channel_id=1, source_target_pairs={{0,1},{1,2},{2,3},{3,4},{4,5},{5,6},{6,7},{7,8},{8,9},{9,10},{10,1... | collective-permute-start | bytes 368648 | tf_op jit(solution)/shard_map/ppermute | solution.py:15
  76.2 2.1 collective-permute-start.7
  78.6 3.9 %collective-permute-done.7 = f32[3,20,2,256]{3,2,1,0:T(2,128)S(1)} collective-permute-done((f32[3,20,2,256]{3,2,1,0:T(2,128)S(1)}, f32[3,20,2,256]{3,2,1,0:T(2,128)S(1)}, u32[]{:S(2)}, u32[]{:S(2)}) %collective-permute-start.7) | collective-permute-done | bytes 122912 | tf_op jit(solution)/shard_map/ppermute | solution.py:18
  82.4 0.9 pad_maximum_fusion
  83.8 1.2 slice_add_fusion.4
  85.0 4.9 %fusion.3 = f32[3,16,64,256]{3,2,1,0:T(8,128)} fusion(f32[3,16,64,256]{3,2,1,0:T(8,128)S(1)} %slice_add_fusion.4), kind=kLoop, calls=%fused_computation.15 | loop fusion | flops 3145728 | bytes 6291456 | tf_op jit(solution)/shard_map/add | solution.py:27
  90.0 5.9 %fusion.33 = f32[16,64,256]{2,1,0:T(8,128)S(1)} fusion(f32[3,16,64,256]{3,2,1,0:T(8,128)} %fusion.3, f32[16,64,256]{2,1,0:T(8,128)S(1)} %slice_add_fusion.13, f32[16,64,256]{2,1,0:T(8,128)S(1)} %fusion.43), kind=kLoop, calls=%fused_computation.82 | loop fusion | flops 6553600 | bytes 6291456 | tf_op jit(solution)/shard_map/mul | solution.py:55
  95.9 6.6 %gather_fusion = f32[2048,256]{1,0:T(8,128)S(1)} fusion(f32[1024,256]{1,0:T(8,128)S(1)} %bitcast.57, s32[2048]{0:T(1024)S(1)} %fusion.54), kind=kCustom, calls=%fused_computation | custom fusion | bytes 4202496 | tf_op jit(solution)/shard_map/gather | solution.py:79
  104.7 0.6 slice.330
  105.8 0.6 slice.331
  106.8 0.6 slice.332
  107.4 0.7 pad_select_fusion.2
  108.1 0.6 slice.333
  110.3 8.9 %scatter_custom_fusion.1 = f32[8192,128]{1,0:T(8,128)} fusion(s32[2048]{0:T(1024)S(1)} %broadcast_select_fusion, f32[]{:T(128)} %constant.18.clone.1, f32[2048,256]{1,0:T(8,128)S(1)} %pad_select_fusion, f32[2048,128]{1,0:T(8,128)S(1)} %slice.335, pred[2048]{0:T(1024)(128)(4,1)S(1)} %get-tuple-element.17), kind=kCustom, calls=%fused_computation.36 | custom fusion | flops 262144 | bytes 6294528
  119.2 10.2 %all-to-all-start.2 = ((f32[32,256,128]{2,1,0:T(8,128)}), f32[32,256,128]{2,1,0:T(8,128)}, u32[]{:S(2)}, u32[]{:S(2)}) async-start(f32[32,256,128]{2,1,0:T(8,128)} %bitcast.62), calls=%async_computation.2 | async-start | bytes 8388608 | tf_op jit(solution)/shard_map/all_to_all | solution.py:99
  129.8 95.9 %all-to-all-done.2 = f32[32,256,128]{2,1,0:T(8,128)} async-done(((f32[32,256,128]{2,1,0:T(8,128)}), f32[32,256,128]{2,1,0:T(8,128)}, u32[]{:S(2)}, u32[]{:S(2)}) %all-to-all-start.2) | async-done | bytes 4194336 | tf_op jit(solution)/shard_map/all_to_all | solution.py:99
  225.7 4.3 %convolution_divide_fusion = f32[16,128]{1,0:T(8,128)} fusion(f32[8192,128]{1,0:T(8,128)} %bitcast.22, f32[8192]{0:T(1024)S(1)} %bitcast.66, f32[16]{0:T(128)S(1)} %iota_add_fusion, f32[16]{0:T(128)S(1)} %broadcast_maximum_fusion), kind=kOutput, calls=%fused_computation.52 | convolution fusion | flops 201459712 | bytes 4235392 | tf_op jit(solution)/shard_map/dot_general | solution.py:104
  (56 shorter events, 7.6 us)
Async XLA Ops:
  0.6 16.1 %copy-start.6 = (s32[2]{0:T(128)S(1)}, s32[2]{0:T(128)}, u32[]{:S(2)}) copy-start(s32[2]{0:T(128)} %constant.79) | copy-start | bytes 28
  0.6 16.2 %copy-start.5 = (s32[2]{0:T(128)S(1)}, s32[2]{0:T(128)}, u32[]{:S(2)}) copy-start(s32[2]{0:T(128)} %constant.82) | copy-start | bytes 28
  0.7 6.1 %copy-start.1 = (s32[2048,1]{0,1:T(1,128)S(1)}, s32[2048,1]{0,1:T(1,128)}, u32[]{:S(2)}) copy-start(s32[2048,1]{0,1:T(1,128)} %param.6) | copy-start | bytes 24580
  0.7 16.3 %copy-start.3 = (s32[2048]{0:T(1024)S(1)}, s32[2048]{0:T(1024)}, u32[]{:S(2)}) copy-start(s32[2048]{0:T(1024)} %param.7) | copy-start | bytes 24580
  0.7 25.0 %all-to-all-start = ((f32[128,8,256]{2,1,0:T(8,128)}), f32[128,8,256]{2,1,0:T(8,128)S(1)}, u32[]{:S(2)}, u32[]{:S(2)}) async-start(f32[128,8,256]{2,1,0:T(8,128)} %param.5), calls=%async_computation | async-start | bytes 2097152 | tf_op jit(solution)/shard_map/all_to_all | solution.py:73
  15.9 26.6 %copy-start.2 = (s32[2048]{0:T(1024)S(1)}, s32[2048]{0:T(1024)}, u32[]{:S(2)}) copy-start(s32[2048]{0:T(1024)} %param.9) | copy-start | bytes 24580
  16.6 36.5 %copy-start.4 = (s32[2048]{0:T(1024)S(1)}, s32[2048]{0:T(1024)}, u32[]{:S(2)}) copy-start(s32[2048]{0:T(1024)} %param.8) | copy-start | bytes 24580
  25.6 93.6 %all-to-all-start.1 = ((f32[32,1,256]{2,1,0:T(1,128)}), f32[32,1,256]{2,1,0:T(1,128)S(1)}, u32[]{:S(2)}, u32[]{:S(2)}) async-start(f32[32,1,256]{2,1,0:T(1,128)} %bitcast.18), calls=%async_computation.1 | async-start | bytes 65536 | tf_op jit(solution)/shard_map/all_to_all | solution.py:100
  37.5 5.0 %collective-permute-start = (f32[1,64,256]{2,1,0:T(8,128)S(1)}, f32[1,64,256]{2,1,0:T(8,128)S(1)}, u32[]{:S(2)}, u32[]{:S(2)}) collective-permute-start(f32[1,64,256]{2,1,0:T(8,128)S(1)} %get-tuple-element.13), channel_id=1, source_target_pairs={{0,32},{32,64},{64,96},{96,128},{128,160},{160,192},{192,224},{1,3... | collective-permute-start | bytes 196616 | tf_op jit(solution)/shard_map/ppermute | solution.py:15
  41.1 5.3 %collective-permute-start.1 = (f32[1,64,256]{2,1,0:T(8,128)S(1)}, f32[1,64,256]{2,1,0:T(8,128)S(1)}, u32[]{:S(2)}, u32[]{:S(2)}) collective-permute-start(f32[1,64,256]{2,1,0:T(8,128)S(1)} %get-tuple-element.14), channel_id=1, source_target_pairs={{32,0},{64,32},{96,64},{128,96},{160,128},{192,160},{224,192},{33,... | collective-permute-start | bytes 196616 | tf_op jit(solution)/shard_map/ppermute | solution.py:18
  46.5 6.6 %collective-permute-start.2 = (f32[18,1,256]{2,1,0:T(1,128)S(1)}, f32[18,1,256]{2,1,0:T(1,128)S(1)}, u32[]{:S(2)}, u32[]{:S(2)}) collective-permute-start(f32[18,1,256]{2,1,0:T(1,128)S(1)} %get-tuple-element.11), channel_id=1, source_target_pairs={{0,1},{1,2},{2,3},{3,4},{4,5},{5,6},{6,7},{7,8},{8,9},{9,10},{10,1... | collective-permute-start | bytes 55304 | tf_op jit(solution)/shard_map/ppermute | solution.py:15
  51.2 5.1 %collective-permute-start.3 = (f32[18,1,256]{2,1,0:T(1,128)S(1)}, f32[18,1,256]{2,1,0:T(1,128)S(1)}, u32[]{:S(2)}, u32[]{:S(2)}) collective-permute-start(f32[18,1,256]{2,1,0:T(1,128)S(1)} %get-tuple-element.10), channel_id=1, source_target_pairs={{1,0},{2,1},{3,2},{4,3},{5,4},{6,5},{7,6},{8,7},{9,8},{10,9},{11,1... | collective-permute-start | bytes 55304 | tf_op jit(solution)/shard_map/ppermute | solution.py:18
  57.2 10.5 %collective-permute-start.4 = (f32[3,2,64,256]{3,2,1,0:T(8,128)S(1)}, f32[3,2,64,256]{3,2,1,0:T(8,128)S(1)}, u32[]{:S(2)}, u32[]{:S(2)}) collective-permute-start(f32[3,2,64,256]{3,2,1,0:T(8,128)S(1)} %get-tuple-element.4), channel_id=1, source_target_pairs={{0,32},{32,64},{64,96},{96,128},{128,160},{160,192},{192,224},{1,3... | collective-permute-start | bytes 1179656 | tf_op jit(solution)/shard_map/ppermute | solution.py:15
  60.3 11.5 %collective-permute-start.5 = (f32[3,2,64,256]{3,2,1,0:T(8,128)S(1)}, f32[3,2,64,256]{3,2,1,0:T(8,128)S(1)}, u32[]{:S(2)}, u32[]{:S(2)}) collective-permute-start(f32[3,2,64,256]{3,2,1,0:T(8,128)S(1)} %get-tuple-element.5), channel_id=1, source_target_pairs={{32,0},{64,32},{96,64},{128,96},{160,128},{192,160},{224,192},{33,... | collective-permute-start | bytes 1179656 | tf_op jit(solution)/shard_map/ppermute | solution.py:18
  71.9 6.6 %collective-permute-start.6 = (f32[3,20,2,256]{3,2,1,0:T(2,128)S(1)}, f32[3,20,2,256]{3,2,1,0:T(2,128)S(1)}, u32[]{:S(2)}, u32[]{:S(2)}) collective-permute-start(f32[3,20,2,256]{3,2,1,0:T(2,128)S(1)} %get-tuple-element.2), channel_id=1, source_target_pairs={{0,1},{1,2},{2,3},{3,4},{4,5},{5,6},{6,7},{7,8},{8,9},{9,10},{10,1... | collective-permute-start | bytes 368648 | tf_op jit(solution)/shard_map/ppermute | solution.py:15
  76.2 6.2 %collective-permute-start.7 = (f32[3,20,2,256]{3,2,1,0:T(2,128)S(1)}, f32[3,20,2,256]{3,2,1,0:T(2,128)S(1)}, u32[]{:S(2)}, u32[]{:S(2)}) collective-permute-start(f32[3,20,2,256]{3,2,1,0:T(2,128)S(1)} %get-tuple-element.3), channel_id=1, source_target_pairs={{1,0},{2,1},{3,2},{4,3},{5,4},{6,5},{7,6},{8,7},{9,8},{10,9},{11,1... | collective-permute-start | bytes 368648 | tf_op jit(solution)/shard_map/ppermute | solution.py:18
  95.9 6.7 %copy-start = (f32[16,64,256]{2,1,0:T(8,128)}, f32[16,64,256]{2,1,0:T(8,128)S(1)}, u32[]{:S(2)}) copy-start(f32[16,64,256]{2,1,0:T(8,128)S(1)} %fusion.33) | copy-start | bytes 3145732
  119.2 106.5 %all-to-all-start.2 = ((f32[32,256,128]{2,1,0:T(8,128)}), f32[32,256,128]{2,1,0:T(8,128)}, u32[]{:S(2)}, u32[]{:S(2)}) async-start(f32[32,256,128]{2,1,0:T(8,128)} %bitcast.62), calls=%async_computation.2 | async-start | bytes 8388608 | tf_op jit(solution)/shard_map/all_to_all | solution.py:99
where the time goes:
time: 232 us; the launch traced here: 230 us
  waiting for transfers between devices  116 us (50%)
  starting transfers between devices  50.4 us (22%)
  other arithmetic  37.7 us (16%)
  local copies, waits for them, and re-layouts  20.1 us (9%)
  matrix products  4.29 us (2%)
    all_to_all x1, waiting for transfers between devices, local(): lax.all_to_all(buffer, 'bulk', split_axis=0, concat_axis=0, tiled=True)  95.9 us
    ppermute x4, starting transfers between devices, padded_2(): lax.ppermute(lax.slice_in_dim(block, block.shape[dim] - width, None, axis...  15.7 us
    ppermute x4, waiting for transfers between devices, padded_2(): lax.ppermute(lax.slice_in_dim(block, 0, width, axis=dim), axis, backward)  15.1 us
    all_to_all x1, starting transfers between devices, local(): lax.all_to_all(labels, 'bulk', split_axis=0, concat_axis=0, tiled=True)  11.7 us
    all_to_all x1, starting transfers between devices, local(): lax.all_to_all(buffer, 'bulk', split_axis=0, concat_axis=0, tiled=True)  10.2 us
    another operation x3, other arithmetic  9.41 us
    unnamed x4, other arithmetic  9.14 us
    unnamed x15, local copies, waits for them, and re-layouts  8.66 us
  transfers between devices with their start and end apart: 11, of which 6 were waited for; matrix products, arithmetic and copies ran while one was open for 25% of the time, Pallas kernels for 0%

commit v1 on v0

v1 whole, which is shorter than its diff:
```python
import functools

import jax
import jax.numpy as jnp
from jax import lax
from jax.experimental import pallas as pl
from jax.experimental.pallas import tpu as pltpu
from jax.sharding import PartitionSpec as P

MESH = pl.DeviceIdType.MESH
F32, BF16 = jnp.float32, jnp.bfloat16
NB, NK = 8, 32
CX, CY, NT, HALF = 16, 64, 256, 128
PATCHES, PATCH, F_DEV = 2048, 128, 16
FAULTS = NK * F_DEV
TRACES = CX * CY
GROUP = 4
GROUPS = CX // GROUP
PIECES = ((0, 10), (10, 4), (14, 4), (18, 4))
FIRST_ROWS = 7
LAST_ROWS = 1
Q = 72
NEAR_C = 80


def split(x):
    hi = x.astype(BF16)
    return hi, (x - hi.astype(F32)).astype(BF16)


def kernel(amp, owner, fault, trace, offset, attr_out, prof_out,
           near, ep, eq, vp, vq, w1, w2, f5, f9, t5, t9, b5, b9, attr_v, attr_bf,
           pick, offs, seg, rows, part, rbuf, cnts, cbuf,
           self_sem, send_sem, recv_sem, hsend_sem, hrecv_sem, out_sem,
           psend_sem, precv_sem, csend_sem, crecv_sem):
    b, k = lax.axis_index("brick"), lax.axis_index("bulk")

    barrier = pltpu.get_barrier_semaphore()
    for d in range(1, NB):
        pl.semaphore_signal(barrier, inc=1, device_id=(lax.rem(b + d, NB), k), device_id_type=MESH)
    for d in range(1, NK):
        pl.semaphore_signal(barrier, inc=1, device_id=(b, lax.rem(k + d, NK)), device_id_type=MESH)

    def for_variant(g, t, act):
        start, count = PIECES[g]
        if g == 0:
            @pl.when(t == 0)
            def _():
                act(count - FIRST_ROWS, FIRST_ROWS)

            @pl.when(t != 0)
            def _():
                act(start, count)
        elif g == GROUPS - 1:
            @pl.when(t == NB - 1)
            def _():
                act(start, LAST_ROWS)

            @pl.when(t != NB - 1)
            def _():
                act(start, count)
        else:
            act(start, count)

    def strip(ref, start, count, s):
        return ref.at[pl.ds(start, count), :, pl.ds(pl.multiple_of(8 + 8 * s, 8), 8), :]

    def block(t, start, count):
        return amp.at[pl.ds(t * CX - 3 + start, count)]

    def self_copy(g, act):
        def go(start, count):
            act(pltpu.make_async_copy(block(b, start, count), strip(near, start, count, b), self_sem.at[g]))
        for_variant(g, b, go)

    for g in range(GROUPS):
        self_copy(g, lambda copy: copy.start())

    @pl.when(b == 0)
    def _():
        near[0:3] = jnp.zeros((3, 2, NEAR_C, HALF), F32)

    @pl.when(b == NB - 1)
    def _():
        near[19:22] = jnp.zeros((3, 2, NEAR_C, HALF), F32)

    @pl.when(k == 0)
    def _():
        near[:, :, 0:8, :] = jnp.zeros((22, 2, 8, HALF), F32)

    @pl.when(k == NK - 1)
    def _():
        near[:, :, 72:80, :] = jnp.zeros((22, 2, 8, HALF), F32)

    pl.semaphore_wait(barrier, NB - 1 + NK - 1)

    peers = [(0, 1), (1, 0), (0, 3), (1, 1), (0, 2), (1, 3), (1, 2)]

    def peer(dx, dy):
        return lax.rem(b // 4 + dx, 2) * 4 + lax.rem(lax.rem(b, 4) + dy, 4)

    def send(g, t, act):
        def go(start, count):
            act(pltpu.make_async_remote_copy(
                src_ref=block(t, start, count), dst_ref=strip(near, start, count, b),
                send_sem=send_sem.at[g, t], recv_sem=recv_sem.at[g, b],
                device_id=(t, k), device_id_type=MESH))
        for_variant(g, t, go)

    def arrived(g, s):
        def go(start, count):
            pltpu.make_async_remote_copy(
                src_ref=block(b, start, count), dst_ref=strip(near, start, count, s),
                send_sem=send_sem.at[g, s], recv_sem=recv_sem.at[g, s],
                device_id=(s, k), device_id_type=MESH).wait_recv()
        for_variant(g, b, go)

    for g in range(GROUPS):
        for dx, dy in peers:
            send(g, peer(dx, dy), lambda copy: copy.start())

    def halo_up(g, act):
        def go(start, count):
            act(pltpu.make_async_remote_copy(
                src_ref=near.at[pl.ds(start, count), :, 64:72, :],
                dst_ref=near.at[pl.ds(start, count), :, 0:8, :],
                send_sem=hsend_sem.at[g, 0], recv_sem=hrecv_sem.at[g, 0],
                device_id=(b, lax.rem(k + 1, NK)), device_id_type=MESH))
        for_variant(g, b, go)

    def halo_down(g, act):
        def go(start, count):
            act(pltpu.make_async_remote_copy(
                src_ref=near.at[pl.ds(start, count), :, 8:16, :],
                dst_ref=near.at[pl.ds(start, count), :, 72:80, :],
                send_sem=hsend_sem.at[g, 1], recv_sem=hrecv_sem.at[g, 1],
                device_id=(b, lax.rem(k + NK - 1, NK)), device_id_type=MESH))
        for_variant(g, b, go)

    row = lax.broadcasted_iota(jnp.int32, (NT, NT), 0)
    col = lax.broadcasted_iota(jnp.int32, (NT, NT), 1)
    near_diag = jnp.abs(row - col)
    for half in range(2):
        b5[half * NT:(half + 1) * NT] = jnp.where(near_diag <= 2, 1.0, 0.0).astype(BF16)
        b9[half * NT:(half + 1) * NT] = jnp.where(near_diag <= 4, 1.0, 0.0).astype(BF16)

    lane = lax.broadcasted_iota(jnp.int32, (HALF, HALF), 1)
    sub = lax.broadcasted_iota(jnp.int32, (HALF, HALF), 0)

    @pl.loop(0, PATCHES // HALF)
    def _(m):
        at = pl.ds(pl.multiple_of(m * HALF, HALF), HALF)
        traces = jnp.broadcast_to(trace[pl.ds(m, 1), :], (HALF, HALF)).T
        for j in range(TRACES // HALF):
            pick[at, j * HALF:(j + 1) * HALF] = jnp.where(traces == lane + j * HALF, 1.0, 0.0).astype(BF16)
        offs[at, :] = jnp.broadcast_to(offset[pl.ds(m, 1), :], (HALF, HALF)).T + lane
        label = jnp.broadcast_to(owner[pl.ds(m, 1), :] * F_DEV + fault[pl.ds(m, 1), :], (HALF, HALF))
        for j in range(FAULTS // HALF):
            seg[j * HALF:(j + 1) * HALF, at] = jnp.where(label == sub + j * HALF, 1.0, 0.0).astype(BF16)

    def count_body(m, total):
        own = jnp.broadcast_to(owner[pl.ds(m, 1), :], (NK, HALF)) == sub[:NK]
        of = jnp.broadcast_to(fault[pl.ds(m, 1), :], (HALF, HALF)) == sub
        return total + lax.dot_general(
            jnp.where(own, 1.0, 0.0).astype(BF16), jnp.where(of, 1.0, 0.0).astype(BF16),
            (((1,), (1,)), ((), ())), preferred_element_type=F32)

    cnts[...] = lax.fori_loop(0, PATCHES // HALF, count_body, jnp.zeros((NK, HALF), F32))

    def count_send(d):
        to = lax.rem(k + d, NK)
        return pltpu.make_async_remote_copy(
            src_ref=cnts.at[pl.ds(to, 1)], dst_ref=cbuf.at[pl.ds(k, 1)],
            send_sem=csend_sem.at[to], recv_sem=crecv_sem.at[k],
            device_id=(b, to), device_id_type=MESH)

    @pl.loop(1, NK)
    def _(d):
        count_send(d).start()

    lanes = lax.broadcasted_iota(jnp.int32, (Q, HALF), 1)

    def energy_row(e):
        low, high = near[e + 1, 0, 6:78, :], near[e + 1, 1, 6:78, :]
        low_r, high_r = pltpu.roll(low, 1, 1), pltpu.roll(high, 1, 1)
        low_l, high_l = pltpu.roll(low, HALF - 1, 1), pltpu.roll(high, HALF - 1, 1)
        first, last = lanes == 0, lanes == HALF - 1
        dt = (
            jnp.where(last, high_l, low_l) - jnp.where(first, 0.0, low_r),
            jnp.where(last, 0.0, high_l) - jnp.where(first, low_r, high_r),
        )
        for h in range(2):
            dx = near[e + 2, h, 6:78, :] - near[e, h, 6:78, :]
            dy = near[e + 1, h, 7:79, :] - near[e + 1, h, 5:77, :]
            lateral = dx * dx + dy * dy
            ep[e, h] = lateral
            eq[e, h] = lateral + dt[h] * dt[h]

    def fields_row(i):
        slot = lax.rem(i, GROUP) * 2
        for h in range(2):
            vp[h] = ep[i, h] + ep[i + 1, h] + ep[i + 2, h] + ep[i + 3, h] + ep[i + 4, h]
            vq[h] = eq[i, h] + eq[i + 1, h] + eq[i + 2, h] + eq[i + 3, h] + eq[i + 4, h]
            a, c, d = near[i + 2, h, 7:79, :], near[i + 3, h, 7:79, :], near[i + 4, h, 7:79, :]
            w1[h] = a + c + d
            w2[h] = a * a + c * c + d * d
        for h in range(2):
            box = [sum(v[h, o:o + CY, :] for o in range(5)) for v in (vp, vq)]
            stack, power = (sum(w[h, o:o + CY, :] for o in range(3)) for w in (w1, w2))
            for target, values in ((f5, box), (f9, [9.0 * power - stack * stack, power])):
                for n in range(2):
                    hi, lo = split(values[n])
                    at = pl.ds(pl.multiple_of((slot + n) * CY, CY), CY)
                    target[at, h * HALF:(h + 1) * HALF] = hi
                    target[at, NT + h * HALF:NT + (h + 1) * HALF] = lo

    def finish_row(i):
        slot = lax.rem(i, GROUP) * 2
        top, low = (pl.ds(pl.multiple_of((slot + n) * CY, CY), CY) for n in range(2))
        value = ((t9[top, :] + 1e-05) * t5[top, :]) / ((9.0 * t9[low, :] + 1e-05) * (t5[low, :] + 4e-05))
        attr_v[i] = value
        hi, lo = split(value)
        at = pl.ds(pl.multiple_of(i * CY, CY), CY)
        attr_bf[at, 0:NT] = hi
        attr_bf[at, NT:2 * NT] = lo

    def out_copy(g):
        at = slice(g * GROUP, (g + 1) * GROUP)
        return pltpu.make_async_copy(attr_v.at[at], attr_out.at[at], out_sem.at[g])

    for g in range(GROUPS):
        self_copy(g, lambda copy: copy.wait())
        for dx, dy in peers:
            arrived(g, peer(dx, dy))

        @pl.when(k != NK - 1)
        def _():
            halo_up(g, lambda copy: copy.start())

        @pl.when(k != 0)
        def _():
            halo_down(g, lambda copy: copy.start())

        @pl.when(k != 0)
        def _():
            halo_up(g, lambda copy: copy.wait_recv())

        @pl.when(k != NK - 1)
        def _():
            halo_down(g, lambda copy: copy.wait_recv())

        e0, e1 = (0, 8) if g == 0 else (4 * g + 4, 4 * g + 8)
        pl.loop(e0, e1)(energy_row)

        @pl.when(k == 0)
        def _():
            ep[e0:e1, :, 0:2, :] = jnp.zeros((e1 - e0, 2, 2, HALF), F32)
            eq[e0:e1, :, 0:2, :] = jnp.zeros((e1 - e0, 2, 2, HALF), F32)

        @pl.when(k == NK - 1)
        def _():
            ep[e0:e1, :, 66:68, :] = jnp.zeros((e1 - e0, 2, 2, HALF), F32)
            eq[e0:e1, :, 66:68, :] = jnp.zeros((e1 - e0, 2, 2, HALF), F32)

        if g in (0, GROUPS - 1):
            edge = 0 if g == 0 else 18

            @pl.when(b == (0 if g == 0 else NB - 1))
            def _():
                ep[edge:edge + 2] = jnp.zeros((2, 2, Q, HALF), F32)
                eq[edge:edge + 2] = jnp.zeros((2, 2, Q, HALF), F32)

        pl.loop(g * GROUP, (g + 1) * GROUP)(fields_row)
        t5[...] = jnp.dot(f5[...], b5[...], preferred_element_type=F32)
        t9[...] = jnp.dot(f9[...], b9[...], preferred_element_type=F32)
        pl.loop(g * GROUP, (g + 1) * GROUP)(finish_row)
        out_copy(g).start()

    chunk = 256

    @pl.loop(0, PATCHES // chunk)
    def _(m):
        at = pl.ds(pl.multiple_of(m * chunk, chunk), chunk)
        picked = jnp.dot(pick[at, :], attr_bf[...], preferred_element_type=F32)
        early = picked[:, 0:HALF] + picked[:, NT:NT + HALF]
        late = picked[:, HALF:NT] + picked[:, NT + HALF:2 * NT]
        index = offs[at, :]
        turn = jnp.bitwise_and(index, HALF - 1)
        taken = jnp.where(
            index < HALF,
            jnp.take_along_axis(early, turn, axis=1, mode="promise_in_bounds"),
            jnp.take_along_axis(late, turn, axis=1, mode="promise_in_bounds"))
        hi, lo = split(taken)
        rows[at, 0:HALF] = hi
        rows[at, HALF:2 * HALF] = lo

    both = jnp.dot(seg[...], rows[...], preferred_element_type=F32)
    part[...] = both[:, 0:HALF] + both[:, HALF:2 * HALF]

    def part_send(d):
        to = lax.rem(k + d, NK)
        return pltpu.make_async_remote_copy(
            src_ref=part.at[pl.ds(pl.multiple_of(to * F_DEV, F_DEV), F_DEV)], dst_ref=rbuf.at[k],
            send_sem=psend_sem.at[to], recv_sem=precv_sem.at[k],
            device_id=(b, to), device_id_type=MESH)

    def part_recv(d):
        source = lax.rem(k + NK - d, NK)
        return pltpu.make_async_remote_copy(
            src_ref=part.at[0:F_DEV], dst_ref=rbuf.at[source],
            send_sem=psend_sem.at[source], recv_sem=precv_sem.at[source],
            device_id=(b, source), device_id_type=MESH)

    def count_recv(d):
        source = lax.rem(k + NK - d, NK)
        return pltpu.make_async_remote_copy(
            src_ref=cnts.at[0:1], dst_ref=cbuf.at[pl.ds(source, 1)],
            send_sem=csend_sem.at[source], recv_sem=crecv_sem.at[source],
            device_id=(b, source), device_id_type=MESH)

    @pl.loop(1, NK)
    def _(d):
        part_send(d).start()

    def count_sum(d, total):
        count_recv(d).wait_recv()
        return total + cbuf[pl.ds(lax.rem(k + NK - d, NK), 1), :]

    number = lax.fori_loop(1, NK, count_sum, cnts[pl.ds(k, 1), :])
    column = jnp.sum(
        jnp.where(lane[:F_DEV] == sub[:F_DEV], jnp.broadcast_to(number, (F_DEV, HALF)), 0.0),
        axis=1, keepdims=True)

    def part_sum(d, total):
        part_recv(d).wait_recv()
        return total + rbuf[lax.rem(k + NK - d, NK)]

    own_part = part[pl.ds(pl.multiple_of(k * F_DEV, F_DEV), F_DEV), :]
    summed = lax.fori_loop(1, NK, part_sum, own_part)
    prof_out[...] = summed / jnp.maximum(column, 1.0)

    for g in range(GROUPS):
        out_copy(g).wait()
        for dx, dy in peers:
            send(g, peer(dx, dy), lambda copy: copy.wait_send())

        @pl.when(k != NK - 1)
        def _():
            halo_up(g, lambda copy: copy.wait_send())

        @pl.when(k != 0)
        def _():
            halo_down(g, lambda copy: copy.wait_send())

    @pl.loop(1, NK)
    def _(d):
        count_send(d).wait_send()
        part_send(d).wait_send()


def local(amp_traces, patch_owner, patch_fault, patch_trace, patch_offset):
    halves = amp_traces.reshape(NB * CX, 8, 2, HALF).transpose(0, 2, 1, 3)
    table = (PATCHES // HALF, HALF)
    vmem = pl.BlockSpec(memory_space=pltpu.VMEM)
    dma = pltpu.SemaphoreType.DMA
    return pl.pallas_call(
        kernel,
        out_shape=(
            jax.ShapeDtypeStruct((CX, CY, NT), F32),
            jax.ShapeDtypeStruct((F_DEV, PATCH), F32),
        ),
        in_specs=[pl.BlockSpec(memory_space=pl.ANY)] + [vmem] * 4,
        out_specs=(pl.BlockSpec(memory_space=pl.ANY), vmem),
        scratch_shapes=[
            pltpu.VMEM((CX + 6, 2, NEAR_C, HALF), F32),
            pltpu.VMEM((CX + 4, 2, Q, HALF), F32),
            pltpu.VMEM((CX + 4, 2, Q, HALF), F32),
            pltpu.VMEM((2, Q, HALF), F32),
            pltpu.VMEM((2, Q, HALF), F32),
            pltpu.VMEM((2, Q, HALF), F32),
            pltpu.VMEM((2, Q, HALF), F32),
            pltpu.VMEM((GROUP * 2 * CY, 2 * NT), BF16),
            pltpu.VMEM((GROUP * 2 * CY, 2 * NT), BF16),
            pltpu.VMEM((GROUP * 2 * CY, NT), F32),
            pltpu.VMEM((GROUP * 2 * CY, NT), F32),
            pltpu.VMEM((2 * NT, NT), BF16),
            pltpu.VMEM((2 * NT, NT), BF16),
            pltpu.VMEM((CX, CY, NT), F32),
            pltpu.VMEM((TRACES, 2 * NT), BF16),
            pltpu.VMEM((PATCHES, TRACES), BF16),
            pltpu.VMEM((PATCHES, HALF), jnp.int32),
            pltpu.VMEM((FAULTS, PATCHES), BF16),
            pltpu.VMEM((PATCHES, 2 * HALF), BF16),
            pltpu.VMEM((FAULTS, PATCH), F32),
            pltpu.VMEM((NK, F_DEV, PATCH), F32),
            pltpu.VMEM((NK, HALF), F32),
            pltpu.VMEM((NK, HALF), F32),
            dma((GROUPS,)),
            dma((GROUPS, NB)),
            dma((GROUPS, NB)),
            dma((GROUPS, 2)),
            dma((GROUPS, 2)),
            dma((GROUPS,)),
            dma((NK,)),
            dma((NK,)),
            dma((NK,)),
            dma((NK,)),
        ],
        compiler_params=pltpu.CompilerParams(collective_id=0, has_side_effects=True),
        name="fault_attribute",
    )(
        halves,
        patch_owner.reshape(table),
        patch_fault.reshape(table),
        patch_trace.reshape(table),
        patch_offset.reshape(table),
    )


def solution(mesh):
    in_specs = (
        P(None, ("bulk", "brick"), None),
        P(("brick", "bulk"), None),
        P(("brick", "bulk")),
        P(("brick", "bulk")),
        P(("brick", "bulk")),
    )
    out_specs = (P("brick", "bulk", None), P(("brick", "bulk"), None))
    return jax.shard_map(local, mesh=mesh, in_specs=in_specs, out_specs=out_specs, check_vma=False)
```

time: 232 us -> 63.7 us (0.27)
  waiting for transfers between devices: 116 us -> 0 us
  Pallas kernels: 0 us -> 60 us
  starting transfers between devices: 50.4 us -> 0 us
  other arithmetic: 37.7 us -> 0 us
  local copies, waits for them, and re-layouts: 20.1 us -> 2.9 us
  matrix products: 4.29 us -> 0 us
    all_to_all x3 -> x0, waiting for transfers between devices: 95.9 us -> none  [the longest x1 95.9 us: local(): lax.all_to_all(buffer, 'bulk', split_axis=0, concat_axis=0, tiled=True)]
    pallas_call x0 -> x1, Pallas kernels: none -> 60 us  [local(): pl.pallas_call(kernel, out_shape=(jax.ShapeDtypeStruct((CX, CY, NT), F32)...]
    all_to_all x3 -> x0, starting transfers between devices: 28.1 us -> none  [the longest x1 11.7 us: local(): lax.all_to_all(labels, 'bulk', split_axis=0, concat_axis=0, tiled=True)]
    ppermute x8 -> x0, starting transfers between devices: 22.3 us -> none  [the longest x4 15.7 us: padded_2(): lax.ppermute(lax.slice_in_dim(block, block.shape[dim] - width, None, axis...]
    ppermute x8 -> x0, waiting for transfers between devices: 20.5 us -> none  [the longest x4 15.1 us: padded_2(): lax.ppermute(lax.slice_in_dim(block, 0, width, axis=dim), axis, backward)]
    another operation x4 -> x0, other arithmetic: 10.3 us -> none
    unnamed x4 -> x0, other arithmetic: 9.14 us -> none
    add x7 -> x0, other arithmetic: 7.06 us -> none  [the longest x5 7.05 us: box_sum(): summed + lax.slice_in_dim(values, offset, offset + length, axis=dimension)]
  transfers between devices with their start and end apart: 11 -> 0, of which waited for: 6 -> 0; matrix products, arithmetic and copies ran while one was open for 25% -> 0% of each run, Pallas kernels for 0% -> 0%
where the time goes in v1:
time: 63.7 us; the launch traced here: 63.6 us
  Pallas kernels  60 us (94%)
  local copies, waits for them, and re-layouts  2.9 us (5%)
  between operations  0.65 us (1%)
    pallas_call x1, Pallas kernels, local(): pl.pallas_call(kernel, out_shape=(jax.ShapeDtypeStruct((CX, CY, NT), F32)...  60 us
    unnamed x4, local copies, waits for them, and re-layouts  2.9 us

profile of v1, /device:TPU:1, one launch (start us, length us, event | category | flops | bytes accessed | tf_op | source)
XLA Modules:
  0.0 63.6 jit_solution(10826245896623433843)
XLA Ops:
  0.6 60.0 %fault_attribute.1 = (f32[16,64,256]{2,1,0:T(8,128)}, f32[16,128]{1,0:T(8,128)}) custom-call(f32[128,2,8,128]{3,2,1,0:T(8,128)} %bitcast.7, s32[16,128]{1,0:T(8,128)} %bitcast.8, s32[16,128]{1,0:T(8,128)} %bitcast.9, s32[16,128]{1,0:T(8,128)} %bitcast.10, s32[16,128]{1,0:T(8,128)} %bitcast.11), custom_call_target="tpu_custom_call" | custom-call | tf_op jit(solution)/shard_map/fault_attribute/pallas_call | solution.py:366
  60.6 0.0 copy-start
  60.7 2.3 %copy.9 = f32[16,64,256]{2,1,0:T(8,128)} copy(f32[16,64,256]{2,1,0:T(8,128)} %get-tuple-element.4) | data formatting | bytes 2097152
  63.0 0.0 copy-done
  63.0 0.6 copy.10
Async XLA Ops:
  60.6 2.3 %copy-start = (f32[16,128]{1,0:T(8,128)S(1)}, f32[16,128]{1,0:T(8,128)}, u32[]{:S(2)}) copy-start(f32[16,128]{1,0:T(8,128)} %get-tuple-element.5) | copy-start | bytes 24580

commit v2 on v1

--- a/solution.py
+++ b/solution.py
@@ -28,10 +28,10 @@
     return hi, (x - hi.astype(F32)).astype(BF16)
 
 
-def kernel(amp, owner, fault, trace, offset, attr_out, prof_out,
-           near, ep, eq, vp, vq, w1, w2, f5, f9, t5, t9, b5, b9, attr_v, attr_bf,
+def kernel(amp, owner_in, fault_in, trace_in, offset_in, attr_out, prof_out,
+           owner, fault, trace, offset, near, ep, eq, vp, vq, w1, w2, f5, f9, t5, t9, b5, b9, attr_bf, picked,
            pick, offs, seg, rows, part, rbuf, cnts, cbuf,
-           self_sem, send_sem, recv_sem, hsend_sem, hrecv_sem, out_sem,
+           index_sem, self_sem, send_sem, recv_sem, hsend_sem, hrecv_sem,
            psend_sem, precv_sem, csend_sem, crecv_sem):
     b, k = lax.axis_index("brick"), lax.axis_index("bulk")
 
@@ -40,6 +40,14 @@
         pl.semaphore_signal(barrier, inc=1, device_id=(lax.rem(b + d, NB), k), device_id_type=MESH)
     for d in range(1, NK):
         pl.semaphore_signal(barrier, inc=1, device_id=(b, lax.rem(k + d, NK)), device_id_type=MESH)
+
+    tables = [
+        pltpu.make_async_copy(source, target, index_sem.at[n])
+        for n, (source, target) in enumerate(
+            ((owner_in, owner), (fault_in, fault), (trace_in, trace), (offset_in, offset)))
+    ]
+    for copy in tables:
+        copy.start()
 
     def for_variant(g, t, act):
         start, count = PIECES[g]
@@ -115,9 +123,12 @@
                 device_id=(s, k), device_id_type=MESH).wait_recv()
         for_variant(g, b, go)
 
-    for g in range(GROUPS):
+    def send_piece(g):
         for dx, dy in peers:
             send(g, peer(dx, dy), lambda copy: copy.start())
+
+    send_piece(0)
+    send_piece(1)
 
     def halo_up(g, act):
         def go(start, count):
@@ -146,6 +157,9 @@
 
     lane = lax.broadcasted_iota(jnp.int32, (HALF, HALF), 1)
     sub = lax.broadcasted_iota(jnp.int32, (HALF, HALF), 0)
+
+    for copy in tables:
+        copy.wait()
 
     @pl.loop(0, PATCHES // HALF)
     def _(m):
@@ -218,17 +232,37 @@
         slot = lax.rem(i, GROUP) * 2
         top, low = (pl.ds(pl.multiple_of((slot + n) * CY, CY), CY) for n in range(2))
         value = ((t9[top, :] + 1e-05) * t5[top, :]) / ((9.0 * t9[low, :] + 1e-05) * (t5[low, :] + 4e-05))
-        attr_v[i] = value
+        attr_out[i] = value
         hi, lo = split(value)
-        at = pl.ds(pl.multiple_of(i * CY, CY), CY)
-        attr_bf[at, 0:NT] = hi
-        attr_bf[at, NT:2 * NT] = lo
-
-    def out_copy(g):
-        at = slice(g * GROUP, (g + 1) * GROUP)
-        return pltpu.make_async_copy(attr_v.at[at], attr_out.at[at], out_sem.at[g])
-
-    for g in range(GROUPS):
+        at = lax.rem(i, GROUP) * CY
+        attr_bf[pl.ds(pl.multiple_of(at, CY), CY), :] = hi
+        attr_bf[pl.ds(pl.multiple_of(GROUP * CY + at, CY), CY), :] = lo
+
+    chunk = 512
+
+    def pick_traces(g):
+        @pl.loop(0, PATCHES // chunk)
+        def _(m):
+            at = pl.ds(pl.multiple_of(m * chunk, chunk), chunk)
+            chosen = pick[at, g * GROUP * CY:(g + 1) * GROUP * CY]
+            found = jnp.dot(jnp.concatenate([chosen, chosen], axis=1), attr_bf[...], preferred_element_type=F32)
+            if g > 0:
+                found = found + picked[at, :]
+            if g < GROUPS - 1:
+                picked[at, :] = found
+                return
+            early, late = found[:, :HALF], found[:, HALF:]
+            index = offs[at, :]
+            turn = jnp.bitwise_and(index, HALF - 1)
+            taken = jnp.where(
+                index < HALF,
+                jnp.take_along_axis(early, turn, axis=1, mode="promise_in_bounds"),
+                jnp.take_along_axis(late, turn, axis=1, mode="promise_in_bounds"))
+            hi, lo = split(taken)
+            rows[at, 0:HALF] = hi
+            rows[at, HALF:2 * HALF] = lo
+
+    def arrive(g):
         self_copy(g, lambda copy: copy.wait())
         for dx, dy in peers:
             arrived(g, peer(dx, dy))
@@ -241,6 +275,10 @@
         def _():
             halo_down(g, lambda copy: copy.start())
 
+        if g + 2 < GROUPS:
+            send_piece(g + 2)
+
+    def compute(g):
         @pl.when(k != 0)
         def _():
             halo_up(g, lambda copy: copy.wait_recv())
@@ -274,25 +312,13 @@
         t5[...] = jnp.dot(f5[...], b5[...], preferred_element_type=F32)
         t9[...] = jnp.dot(f9[...], b9[...], preferred_element_type=F32)
         pl.loop(g * GROUP, (g + 1) * GROUP)(finish_row)
-        out_copy(g).start()
-
-    chunk = 256
-
-    @pl.loop(0, PATCHES // chunk)
-    def _(m):
-        at = pl.ds(pl.multiple_of(m * chunk, chunk), chunk)
-        picked = jnp.dot(pick[at, :], attr_bf[...], preferred_element_type=F32)
-        early = picked[:, 0:HALF] + picked[:, NT:NT + HALF]
-        late = picked[:, HALF:NT] + picked[:, NT + HALF:2 * NT]
-        index = offs[at, :]
-        turn = jnp.bitwise_and(index, HALF - 1)
-        taken = jnp.where(
-            index < HALF,
-            jnp.take_along_axis(early, turn, axis=1, mode="promise_in_bounds"),
-            jnp.take_along_axis(late, turn, axis=1, mode="promise_in_bounds"))
-        hi, lo = split(taken)
-        rows[at, 0:HALF] = hi
-        rows[at, HALF:2 * HALF] = lo
+        pick_traces(g)
+
+    for g in range(GROUPS):
+        arrive(g)
+        if g > 0:
+            compute(g - 1)
+    compute(GROUPS - 1)
 
     both = jnp.dot(seg[...], rows[...], preferred_element_type=F32)
     part[...] = both[:, 0:HALF] + both[:, HALF:2 * HALF]
@@ -340,7 +366,6 @@
     prof_out[...] = summed / jnp.maximum(column, 1.0)
 
     for g in range(GROUPS):
-        out_copy(g).wait()
         for dx, dy in peers:
             send(g, peer(dx, dy), lambda copy: copy.wait_send())
 
@@ -366,12 +391,16 @@
     return pl.pallas_call(
         kernel,
         out_shape=(
-            jax.ShapeDtypeStruct((CX, CY, NT), F32),
-            jax.ShapeDtypeStruct((F_DEV, PATCH), F32),
+            pltpu.VMEM((CX, CY, NT), F32),
+            pltpu.VMEM((F_DEV, PATCH), F32),
         ),
-        in_specs=[pl.BlockSpec(memory_space=pl.ANY)] + [vmem] * 4,
-        out_specs=(pl.BlockSpec(memory_space=pl.ANY), vmem),
+        in_specs=[pl.BlockSpec(memory_space=pl.ANY)] * 5,
+        out_specs=(vmem, vmem),
         scratch_shapes=[
+            pltpu.VMEM(table, jnp.int32),
+            pltpu.VMEM(table, jnp.int32),
+            pltpu.VMEM(table, jnp.int32),
+            pltpu.VMEM(table, jnp.int32),
             pltpu.VMEM((CX + 6, 2, NEAR_C, HALF), F32),
             pltpu.VMEM((CX + 4, 2, Q, HALF), F32),
             pltpu.VMEM((CX + 4, 2, Q, HALF), F32),
@@ -385,8 +414,8 @@
             pltpu.VMEM((GROUP * 2 * CY, NT), F32),
             pltpu.VMEM((2 * NT, NT), BF16),
             pltpu.VMEM((2 * NT, NT), BF16),
-            pltpu.VMEM((CX, CY, NT), F32),
-            pltpu.VMEM((TRACES, 2 * NT), BF16),
+            pltpu.VMEM((2 * GROUP * CY, NT), BF16),
+            pltpu.VMEM((PATCHES, NT), F32),
             pltpu.VMEM((PATCHES, TRACES), BF16),
             pltpu.VMEM((PATCHES, HALF), jnp.int32),
             pltpu.VMEM((FAULTS, PATCHES), BF16),
@@ -395,12 +424,12 @@
             pltpu.VMEM((NK, F_DEV, PATCH), F32),
             pltpu.VMEM((NK, HALF), F32),
             pltpu.VMEM((NK, HALF), F32),
+            dma((4,)),
             dma((GROUPS,)),
             dma((GROUPS, NB)),
             dma((GROUPS, NB)),
             dma((GROUPS, 2)),
             dma((GROUPS, 2)),
-            dma((GROUPS,)),
             dma((NK,)),
             dma((NK,)),
             dma((NK,)),

time: 63.7 us -> 51.8 us (0.81)
  Pallas kernels: 60 us -> 49.5 us
  local copies, waits for them, and re-layouts: 2.9 us -> 1.57 us
    pallas_call x1, Pallas kernels: 60 us -> 49.5 us  [local(): pl.pallas_call(kernel, out_shape=(pltpu.VMEM((CX, CY, NT), F32), pltpu.VM...]
    unnamed x4 -> x2, local copies, waits for them, and re-layouts: 2.9 us -> 1.57 us
where the time goes in v2:
time: 51.8 us; the launch traced here: 51.7 us
  Pallas kernels  49.5 us (96%)
  local copies, waits for them, and re-layouts  1.57 us (3%)
  between operations  0.64 us (1%)
    pallas_call x1, Pallas kernels, local(): pl.pallas_call(kernel, out_shape=(pltpu.VMEM((CX, CY, NT), F32), pltpu.VM...  49.5 us
    unnamed x2, local copies, waits for them, and re-layouts  1.57 us

profile of v2, /device:TPU:1, one launch (start us, length us, event | category | flops | bytes accessed | tf_op | source)
XLA Modules:
  0.0 51.7 jit_solution(11970296803752550058)
XLA Ops:
  0.6 49.5 %fault_attribute.1 = (f32[16,64,256]{2,1,0:T(8,128)S(1)}, f32[16,128]{1,0:T(8,128)S(1)}) custom-call(f32[128,2,8,128]{3,2,1,0:T(8,128)} %bitcast.7, s32[16,128]{1,0:T(8,128)} %bitcast.8, s32[16,128]{1,0:T(8,128)} %bitcast.9, s32[16,128]{1,0:T(8,128)} %bitcast.10, s32[16,128]{1,0:T(8,128)} %bitcast.11), custom_call_target="tpu_custom_call" | custom-call | tf_op jit(solution)/shard_map/fault_attribute/pallas_call | solution.py:391
  50.2 1.0 %copy.9 = f32[16,64,256]{2,1,0:T(8,128)} copy(f32[16,64,256]{2,1,0:T(8,128)S(1)} %get-tuple-element.2) | data formatting | bytes 2097152
  51.1 0.6 %copy.10 = f32[16,128]{1,0:T(8,128)} copy(f32[16,128]{1,0:T(8,128)S(1)} %get-tuple-element.3) | data formatting | bytes 16384
